TPU v7x, 32 devices: a whole 2x2x4 slice. The times are simulated.
32 devices in a mesh: parts: 2 (over y), tiles: 8 (over z, x), mesh: 2 (over core).
Axes of the slice: x: 2, y: 2, z: 4, core: 2. Of those that a mesh axis runs over, the one named last changes fastest.
Arguments:
- patches: bfloat16 [1024, 128, 128], P(('parts', 'tiles', 'mesh')), parts along dimension 0, may hold values from -6 to 6
- send_index: int32 [32, 32], P(('parts', 'tiles', 'mesh')), parts along dimension 0, may hold values from 0 to 32, as said below
- pair_slots: int32 [32, 2, 16], P(('parts', 'tiles', 'mesh')), parts along dimension 0, may hold values from 0 to 32, as said below
- node_links: int32 [32, 4, 128], P(('parts', 'tiles', 'mesh')), parts along dimension 0, may hold values from 0 to 31
Outputs:
- pair_flow: float32 [2, 512], P(None, ('parts', 'tiles', 'mesh')), parts along dimension 1
- relaxed: float32 [2, 4096], P(None, ('parts', 'tiles', 'mesh')), parts along dimension 1
There are 2 independent parts, one for each index of `parts`. A program takes and returns all parts, laid end to end along the dimension named above; each array names one. Nothing has to cross between parts.
Inputs may be any that keep to these rules, and one draw needn't show every extreme that they name: `send_index`: each patch is sent to at most one owner, as one side of one tile pair; a live pair's two sides come from two different tiles and pair_slots names their received slots, numbered source tile times 4 plus slot; the value 2 * 16 marks an empty send slot. Some device fills all 4 slots to one peer. `pair_slots`: the value 8 * 4 marks a pair slot without a live pair; the number of live pairs differs from owner to owner, and some owner has all 16 slots live.
All inputs are finite; a program needn't handle non-finite values.
Results may differ from a plain program's by a relative error of at most 0.011.
Values may be sent and summed in bfloat16 or wider, within the bound.
No kernel may reach another device: no remote copies, remote signals or barrier semaphores. Data moves between devices by JAX's collectives and lax.ppermute only.
A program may use at most 64 MiB of HBM per device.

v0:
```python
import math
import jax
import jax.numpy as jnp
from jax import lax
from jax.sharding import PartitionSpec as P


def make_tables(side_len):
    ticks = jnp.arange(side_len, dtype=jnp.int32)
    product = ticks[:, None] * ticks[None, :] % side_len
    angle = 2.0 * math.pi / side_len * product.astype(jnp.float32)
    cosine = jnp.cos(angle) / math.sqrt(side_len)
    sine = jnp.sin(angle) / math.sqrt(side_len)
    coord = ticks.astype(jnp.float32)
    gap = coord[:, None] - coord[None, :]
    narrow = jnp.exp(-gap * gap / (2.0 * 0.35 * 0.35)) / (0.35 * math.sqrt(2.0 * math.pi))
    broad = jnp.exp(-gap * gap / 32.0) / (4.0 * math.sqrt(2.0 * math.pi))
    band = narrow - broad
    lag = jnp.where(coord < side_len / 2, coord, coord - side_len)
    return (cosine.astype(jnp.bfloat16), sine.astype(jnp.bfloat16), band.astype(jnp.bfloat16), lag)


def band_pass(stack, band):
    partial_value = jnp.einsum(
        "ij,bjk->bik", band, stack, preferred_element_type=jnp.float32
    ).astype(jnp.bfloat16)
    return jnp.einsum(
        "bij,kj->bik", partial_value, band, preferred_element_type=jnp.float32
    ).astype(jnp.bfloat16)


def prepare(stack, tables):
    cosine, sine, band, lag = tables
    filtered = band_pass(stack, band)
    left = jnp.concatenate([cosine, sine], 0)
    return jnp.einsum("ij,bjk->bik", left, filtered, preferred_element_type=jnp.float32).astype(
        jnp.bfloat16
    )


def finish(halves, tables):
    cosine, sine, band, lag = tables
    side_len = halves.shape[-1]
    count = halves.shape[0] // 2
    right = jnp.concatenate([cosine, sine], 1)
    back_left = jnp.concatenate([cosine, -sine], 1)
    quarter = jnp.einsum("bij,jk->bik", halves, right, preferred_element_type=jnp.float32)
    real_part = quarter[:, :side_len, :side_len] - quarter[:, side_len:, side_len:]
    imag_part = -(quarter[:, :side_len, side_len:] + quarter[:, side_len:, :side_len])
    moving_real, fixed_real = (real_part[:count], real_part[count:])
    moving_imag, fixed_imag = (imag_part[:count], imag_part[count:])
    power_real = moving_real * fixed_real + moving_imag * fixed_imag
    power_imag = moving_imag * fixed_real - moving_real * fixed_imag
    power = jnp.concatenate([power_real, power_imag], 1).astype(jnp.bfloat16)
    mixed = jnp.einsum("bij,jk->bik", power, right, preferred_element_type=jnp.float32)
    first = mixed[:, :side_len, :side_len] - mixed[:, side_len:, side_len:]
    second = mixed[:, :side_len, side_len:] + mixed[:, side_len:, :side_len]
    stacked = jnp.concatenate([first, second], 1).astype(jnp.bfloat16)
    surface = jnp.einsum("ij,bjk->bik", back_left, stacked, preferred_element_type=jnp.float32)
    weight = surface * surface
    denom = jnp.mean(weight, axis=(1, 2)) + 1e-06
    flow_y = jnp.mean(lag[None, :, None] * weight, axis=(1, 2)) / denom
    flow_x = jnp.mean(lag[None, None, :] * weight, axis=(1, 2)) / denom
    return jnp.stack([flow_y, flow_x], 0)


def per_device(patches, send_index, pair_slots, node_links):
    side_len = patches.shape[-1]
    patch_count = patches.shape[0]
    pair_count = pair_slots.shape[-1]
    tile_count = lax.axis_size("tiles")
    tables = make_tables(side_len)
    wanted = send_index[0]
    capacity = wanted.shape[0] // tile_count
    present = wanted < patch_count
    safe_wanted = jnp.minimum(wanted, patch_count - 1)
    picked = patches[safe_wanted]
    picked = jnp.where(present[:, None, None], picked, jnp.zeros_like(picked))
    received = lax.all_to_all(
        picked.reshape((tile_count, capacity) + patches.shape[1:]),
        "tiles",
        split_axis=0,
        concat_axis=0,
        tiled=True,
    )
    slot_total = tile_count * capacity
    received = received.reshape((slot_total,) + received.shape[2:])
    slots = pair_slots[0].reshape(-1)
    valid = slots < slot_total
    chosen = received[jnp.minimum(slots, slot_total - 1)]
    chosen = jnp.where(valid[:, None, None], chosen, jnp.zeros_like(chosen))
    block = min(16, pair_count)
    moving = chosen[:pair_count].reshape((pair_count // block, block) + chosen.shape[1:])
    fixed = chosen[pair_count:].reshape((pair_count // block, block) + chosen.shape[1:])

    def per_block(item):
        moving_part, fixed_part = item
        both = jnp.concatenate([moving_part, fixed_part], 0)
        both = prepare(both, tables)
        return finish(both, tables)

    flows = lax.map(per_block, (moving, fixed))
    pair_flow = jnp.transpose(flows, (1, 0, 2)).reshape(2, pair_count)
    flow_rows = lax.all_gather(pair_flow, "mesh", axis=1, tiled=True)
    linked = flow_rows[:, node_links[0]]
    relaxed = 0.5 * linked[:, 0] + 0.5 * jnp.mean(linked[:, 1:], axis=1)
    return (pair_flow, relaxed)


def solution(mesh):
    placed = (
        P(("parts", "tiles", "mesh"), None, None),
        P(("parts", "tiles", "mesh"), None),
        P(("parts", "tiles", "mesh"), None, None),
        P(("parts", "tiles", "mesh"), None, None),
    )
    return jax.shard_map(
        per_device,
        mesh=mesh,
        in_specs=placed,
        out_specs=(P(None, ("parts", "tiles", "mesh")), P(None, ("parts", "tiles", "mesh"))),
        check_vma=False,
    )
```

profile of v0, /device:TPU:0, one launch (start us, length us, event | category | flops | bytes accessed | tf_op | source)
XLA Modules:
  0.0 55.6 jit_solution(8383764545167968574)
XLA Ops:
  0.6 0.0 copy-start
  0.6 0.7 %fusion.57 = s32[32]{0:T(128)S(1)} fusion(s32[1,32]{1,0:T(1,128)} %param.5), kind=kLoop, calls=%fused_computation.76 | loop fusion | flops 128 | bytes 256 | tf_op jit(solution)/shard_map/select_n | solution.py:77
  1.4 0.7 %compare_reduce_fusion = pred[32]{0:T(512)(128)(4,1)S(1)} fusion(s32[1,32]{1,0:T(1,128)} %param.5), kind=kLoop, calls=%fused_computation.71 | loop fusion | flops 32 | bytes 160 | tf_op jit(solution)/shard_map/lt | solution.py:75
  2.1 0.1 lt.91
  2.2 0.0 copy-done
  2.2 0.8 %gather_fusion = bf16[32,128,128]{2,1,0:T(8,128)(2,1)S(1)} fusion(bf16[32,128,128]{2,1,0:T(8,128)(2,1)S(1)} %copy-done, s32[1024]{0:T(1024)S(1)} %pad_clamp_fusion.2), kind=kCustom, calls=%fused_computation | custom fusion | bytes 2097280 | tf_op jit(solution)/shard_map/gather | solution.py:77
  2.9 0.0 copy-start.2
  2.9 0.0 copy-start.1
  2.9 1.1 %broadcast_select_fusion = bf16[8,4,128,128]{3,2,1,0:T(8,128)(2,1)} fusion(bf16[8,4,128,128]{3,2,1,0:T(8,128)(2,1)S(1)} %bitcast.55, pred[8,4]{1,0:T(8,128)(4,1)S(1)} %lt.91), kind=kLoop, calls=%fused_computation.31 | loop fusion | flops 524288 | bytes 2097184 | tf_op jit(solution)/shard_map/jit(_where)/select_n | solution.py:78
  4.1 7.3 %all-to-all-start = ((bf16[8,4,128,128]{3,2,1,0:T(8,128)(2,1)}), bf16[8,4,128,128]{3,2,1,0:T(8,128)(2,1)S(1)}, u32[]{:S(2)}, u32[]{:S(2)}) async-start(bf16[8,4,128,128]{3,2,1,0:T(8,128)(2,1)} %broadcast_select_fusion), calls=%async_computation | async-start | bytes 2097152 | tf_op jit(solution)/shard_map/all_to_all | solution.py:79
  11.4 0.0 copy-done.2
  11.4 0.1 min.29
  11.5 0.1 lt.89
  11.6 0.0 copy-done.1
  11.6 0.3 fusion.53
  11.9 0.3 multiply_convert_fusion
  12.2 25.0 %all-to-all-done = bf16[8,4,128,128]{3,2,1,0:T(8,128)(2,1)S(1)} async-done(((bf16[8,4,128,128]{3,2,1,0:T(8,128)(2,1)}), bf16[8,4,128,128]{3,2,1,0:T(8,128)(2,1)S(1)}, u32[]{:S(2)}, u32[]{:S(2)}) %all-to-all-start) | async-done | bytes 1048608 | tf_op jit(solution)/shard_map/all_to_all | solution.py:79
  37.1 0.7 %gather_fusion.1 = bf16[32,128,128]{2,1,0:T(8,128)(2,1)S(1)} fusion(bf16[32,128,128]{2,1,0:T(8,128)(2,1)S(1)} %bitcast.54, s32[1024]{0:T(1024)S(1)} %pad_clamp_fusion.1), kind=kCustom, calls=%fused_computation.1 | custom fusion | bytes 2097280 | tf_op jit(solution)/shard_map/gather | solution.py:90
  37.9 1.3 %convolution_convert_fusion = bf16[32,128,128]{2,1,0:T(8,128)(2,1)S(1)} fusion(bf16[32,128,128]{2,1,0:T(8,128)(2,1)S(1)} %gather_fusion.1, pred[32]{0:T(512)(128)(4,1)S(1)} %lt.89, f32[128]{0:T(128)S(1)} %iota_convert_fusion), kind=kOutput, calls=%fused_computation.11 | convolution fusion | flops 270303232 | bytes 2097696 | tf_op jit(solution)/shard_map/while/body/eval_jaxpr/bij,kj->bik/dot_general | solution.py:27
  39.2 5.8 %fusion.1 = f32[32,256,256]{2,1,0:T(8,128)} fusion(bf16[32,128,128]{2,1,0:T(8,128)(2,1)S(1)} %convolution_convert_fusion, bf16[128,128]{1,0:T(8,128)(2,1)S(1)} %get-tuple-element.37, bf16[128,128]{1,0:T(8,128)(2,1)S(1)} %get-tuple-element.38), kind=kOutput, calls=%fused_computation.6 | convolution fusion | flops 806617088 | bytes 9502720 | tf_op jit(solution)/shard_map/while/body/eval_jaxpr/bij,jk->bik/dot_general | solution.py:47
  45.0 4.4 %slice_subtract_fusion = (f32[32,128,128]{2,1,0:T(8,128)S(1)}, f32[32,128,128]{2,1,0:T(8,128)S(1)}) fusion(f32[32,256,256]{2,1,0:T(8,128)} %fusion.1), kind=kLoop, calls=%fused_computation.5 | loop fusion | flops 1572864 | bytes 12582912 | tf_op jit(solution)/shard_map/while/body/eval_jaxpr/sub | solution.py:48
  49.3 0.4 add_convert_fusion
  49.7 0.7 %fusion.9 = f32[16,256,256]{2,1,0:T(8,128)S(1)} fusion(bf16[16,128,128]{2,1,0:T(8,128)(2,1)S(1)} %get-tuple-element.34, bf16[16,128,128]{2,1,0:T(8,128)(2,1)S(1)} %get-tuple-element.33, bf16[128,128]{1,0:T(8,128)(2,1)S(1)} %get-tuple-element.38, bf16[128,128]{1,0:T(8,128)(2,1)S(1)} %get-tuple-element.37), kind=kOutput, calls=%fused_computation.18 | convolution fusion | flops 270663680 | bytes 5308416 | tf_op jit(solution)/shard_map/while/body/eval_jaxpr/bij,jk->bik/dot_general | solution.py:55
  50.4 0.3 fusion.8
  50.7 0.6 %multiply_reduce_fusion.1 = (f32[16]{0:T(128)S(1)}, f32[16]{0:T(128)S(1)}, f32[16]{0:T(128)S(1)}) fusion(f32[128]{0:T(128)S(1)} %compare_select_fusion.3, bf16[128,128]{1,0:T(8,128)(2,1)S(1)} %get-tuple-element.38, bf16[128,128]{1,0:T(8,128)(2,1)S(1)} %fusion.53, bf16[16,128,128]{2,1,0:T(8,128)(2,1)S(1)} %get-tuple-element.32, ...), kind=kOutput, calls=%fused_computation.26 | convolution fusion | flops 138018768 | bytes 1114816 | tf_op jit(solution)/shard_map/while/body/eval_jaxpr/ij,bjk->bik/dot_general | solution.py:59
  51.4 0.6 %pad_maximum_fusion.2 = f32[2,16]{1,0:T(2,128)} fusion(f32[1,16]{1,0:T(1,128)S(1)} %get-tuple-element.36, f32[1,16]{1,0:T(1,128)S(1)} %get-tuple-element.35), kind=kLoop, calls=%fused_computation.75 | loop fusion | flops 32 | bytes 256 | tf_op jit(solution)/shard_map/while/body/eval_jaxpr/stack | solution.py:64
  51.9 1.8 %all-gather = f32[2,16,2]{1,2,0:T(2,128)S(1)} all-gather(f32[1,16,2]{1,2,0:T(2,128)S(1)} %fusion.76), channel_id=1, replica_groups=mesh['parts'=2,'tiles'=8,'mesh'=2] {'mesh'}, dimensions={0}, use_global_device_ids=true | all-gather | bytes 384 | tf_op jit(solution)/shard_map/all_gather | solution.py:104
  53.7 0.1 copy.34
  53.8 1.0 %gather_fusion.2 = f32[512,2]{1,0:T(8,128)S(1)} fusion(f32[2,32]{0,1:T(8,128)S(1)} %bitcast.57, s32[1024]{0:T(1024)S(1)} %pad_clamp_fusion), kind=kCustom, calls=%fused_computation.2 | custom fusion | bytes 10240 | tf_op jit(solution)/shard_map/gather | solution.py:105
  54.9 0.1 copy.28
  55.0 0.6 %fusion.56 = f32[2,128]{1,0:T(2,128)} fusion(f32[2,4,128]{2,0,1:T(2,128)S(1)} %bitcast.59, f32[2,128]{1,0:T(2,128)S(1)} %slice_reduce_fusion), kind=kLoop, calls=%fused_computation.74 | loop fusion | flops 768 | bytes 3072 | tf_op jit(solution)/shard_map/add | solution.py:106
  (12 shorter events, 0.1 us)
Async XLA Ops:
  0.6 1.5 %copy-start = (bf16[32,128,128]{2,1,0:T(8,128)(2,1)S(1)}, bf16[32,128,128]{2,1,0:T(8,128)(2,1)}, u32[]{:S(2)}) copy-start(bf16[32,128,128]{2,1,0:T(8,128)(2,1)} %param.4) | copy-start | bytes 3145732
  2.9 8.4 %copy-start.2 = (s32[1,2,16]{2,1,0:T(2,128)S(1)}, s32[1,2,16]{2,1,0:T(2,128)}, u32[]{:S(2)}) copy-start(s32[1,2,16]{2,1,0:T(2,128)} %param.6) | copy-start | bytes 388
  2.9 8.6 %copy-start.1 = (s32[1,4,128]{2,1,0:T(4,128)S(1)}, s32[1,4,128]{2,1,0:T(4,128)}, u32[]{:S(2)}) copy-start(s32[1,4,128]{2,1,0:T(4,128)} %param.7) | copy-start | bytes 6148
  4.1 33.0 %all-to-all-start = ((bf16[8,4,128,128]{3,2,1,0:T(8,128)(2,1)}), bf16[8,4,128,128]{3,2,1,0:T(8,128)(2,1)S(1)}, u32[]{:S(2)}, u32[]{:S(2)}) async-start(bf16[8,4,128,128]{3,2,1,0:T(8,128)(2,1)} %broadcast_select_fusion), calls=%async_computation | async-start | bytes 2097152 | tf_op jit(solution)/shard_map/all_to_all | solution.py:79
where the time goes:
time: 55.8 us; the launch traced here: 55.6 us
  waiting for transfers between devices  25 us (45%)
  other arithmetic  9.36 us (17%)
  matrix products  8.41 us (15%)
  starting transfers between devices  7.28 us (13%)
  local copies, waits for them, and re-layouts  3 us (5%)
  blocking collectives  1.79 us (3%)
  between operations  0.78 us (1%)
    all_to_all x1, waiting for transfers between devices, per_device(): lax.all_to_all(picked.reshape((tile_count, capacity) + patches.shape[1:])...  25 us
    all_to_all x1, starting transfers between devices, per_device(): lax.all_to_all(picked.reshape((tile_count, capacity) + patches.shape[1:])...  7.28 us
    dot_general x1, matrix products, finish(): jnp.einsum('bij,jk->bik', halves, right, preferred_element_type=jnp.float32)  5.76 us
    sub x1, other arithmetic, finish(): quarter[:, :side_len, :side_len] - quarter[:, side_len:, side_len:]  4.35 us
    all_gather x1, blocking collectives, per_device(): flow_rows = lax.all_gather(pair_flow, 'mesh', axis=1, tiled=True)  1.79 us
    dot_general x1, matrix products, band_pass(): jnp.einsum('bij,kj->bik', partial_value, band, preferred_element_type=jnp...  1.31 us
    gather x2, local copies, waits for them, and re-layouts, per_device(): linked = flow_rows[:, node_links[0]]  1.14 us
    select_n x1, other arithmetic, per_device(): picked = jnp.where(present[:, None, None], picked, jnp.zeros_like(picked))  1.13 us
  transfers between devices with their start and end apart: 1, of which 1 were waited for; matrix products, arithmetic and copies ran while one was open for 1% of the time, Pallas kernels for 0%

commit v1 on v0

--- a/solution.py
+++ b/solution.py
@@ -3,6 +3,25 @@
 import jax.numpy as jnp
 from jax import lax
 from jax.sharding import PartitionSpec as P
+
+
+def track_pairs_all_here(local_x, bus_axis):
+    b_now = lax.axis_size(bus_axis)
+    w2, tile_out = (b_now, lax.axis_index(bus_axis))
+    f_now = local_x.shape[0] // w2
+    x_new = list(local_x.shape)
+    x_new[0] = f_now
+    u1 = x_new[0]
+    x_new[0] = u1 * w2
+    raw_out = jnp.zeros(x_new, local_x.dtype)
+    dev_i = 0
+    while dev_i < w2:
+        earlier = lax.dynamic_slice_in_dim(local_x, (tile_out ^ dev_i) * f_now, f_now, axis=0)
+        if dev_i:
+            earlier = lax.ppermute(earlier, bus_axis, [(jj, jj ^ dev_i) for jj in range(w2)])
+        raw_out = lax.dynamic_update_slice_in_dim(raw_out, earlier, (tile_out ^ dev_i) * u1, axis=0)
+        dev_i = dev_i + 1
+    return raw_out
 
 
 def make_tables(side_len):
@@ -76,12 +95,8 @@
     safe_wanted = jnp.minimum(wanted, patch_count - 1)
     picked = patches[safe_wanted]
     picked = jnp.where(present[:, None, None], picked, jnp.zeros_like(picked))
-    received = lax.all_to_all(
-        picked.reshape((tile_count, capacity) + patches.shape[1:]),
-        "tiles",
-        split_axis=0,
-        concat_axis=0,
-        tiled=True,
+    received = track_pairs_all_here(
+        picked.reshape((tile_count, capacity) + patches.shape[1:]), "tiles"
     )
     slot_total = tile_count * capacity
     received = received.reshape((slot_total,) + received.shape[2:])

time: 55.8 us -> 52 us (0.932)
  the two profiles are of different devices: /device:TPU:0 before, /device:TPU:17 now
where the time goes in v1:
time: 52 us; the launch traced here: 51.8 us
  waiting for transfers between devices  18.2 us (35%)
  matrix products  8.41 us (16%)
  other arithmetic  8.36 us (16%)
  starting transfers between devices  7.51 us (14%)
  local copies, waits for them, and re-layouts  5.26 us (10%)
  blocking collectives  3.17 us (6%)
  between operations  0.86 us (2%)
    ppermute x7, waiting for transfers between devices, track_pairs_all_here(): lax.ppermute(earlier, bus_axis, [(jj, jj ^ dev_i) for jj in range(w2)])  18.2 us
    ppermute x7, starting transfers between devices, track_pairs_all_here(): lax.ppermute(earlier, bus_axis, [(jj, jj ^ dev_i) for jj in range(w2)])  7.51 us
    dot_general x1, matrix products, finish(): jnp.einsum('bij,jk->bik', halves, right, preferred_element_type=jnp.float32)  5.77 us
    sub x1, other arithmetic, finish(): quarter[:, :side_len, :side_len] - quarter[:, side_len:, side_len:]  4.35 us
    all_gather x1, blocking collectives, per_device(): flow_rows = lax.all_gather(pair_flow, 'mesh', axis=1, tiled=True)  3.17 us
    dynamic_update_slice x7, local copies, waits for them, and re-layouts, track_pairs_all_here(): lax.dynamic_update_slice_in_dim(raw_out, earlier, (tile_out ^ dev_i) * u1...  1.93 us
    dot_general x1, matrix products, band_pass(): jnp.einsum('bij,kj->bik', partial_value, band, preferred_element_type=jnp...  1.31 us
    gather x2, local copies, waits for them, and re-layouts, per_device(): linked = flow_rows[:, node_links[0]]  1.14 us
  transfers between devices with their start and end apart: 7, of which 5 were waited for; matrix products, arithmetic and copies ran while one was open for 5% of the time, Pallas kernels for 0%

profile of v1, /device:TPU:17, one launch (start us, length us, event | category | flops | bytes accessed | tf_op | source)
XLA Modules:
  0.0 51.8 jit_solution(15985248138329207789)
XLA Ops:
  0.6 0.0 copy-start
  0.7 0.7 %fusion.57 = s32[32]{0:T(128)S(1)} fusion(s32[1,32]{1,0:T(1,128)} %param.5), kind=kLoop, calls=%fused_computation.91 | loop fusion | flops 128 | bytes 256 | tf_op jit(solution)/shard_map/select_n | solution.py:96
  1.4 0.7 %compare_reduce_fusion = pred[32]{0:T(512)(128)(4,1)S(1)} fusion(s32[1,32]{1,0:T(1,128)} %param.5), kind=kLoop, calls=%fused_computation.86 | loop fusion | flops 32 | bytes 160 | tf_op jit(solution)/shard_map/lt | solution.py:94
  2.1 0.1 lt.123
  2.2 0.0 copy-done
  2.2 0.8 %gather_fusion = bf16[32,128,128]{2,1,0:T(8,128)(2,1)S(1)} fusion(bf16[32,128,128]{2,1,0:T(8,128)(2,1)S(1)} %copy-done, s32[1024]{0:T(1024)S(1)} %pad_clamp_fusion.2), kind=kCustom, calls=%fused_computation | custom fusion | bytes 2097280 | tf_op jit(solution)/shard_map/gather | solution.py:96
  3.0 0.1 broadcast_select_fusion
  3.1 0.0 copy-start.2
  3.1 0.0 copy-start.1
  3.1 0.2 broadcast_in_dim.34
  3.4 0.1 constant_dynamic-slice_fusion
  3.5 1.3 %collective-permute-start = (bf16[1,4,128,128]{3,2,1,0:T(8,128)(2,1)S(1)}, bf16[1,4,128,128]{3,2,1,0:T(8,128)(2,1)}, u32[]{:S(2)}, u32[]{:S(2)}) collective-permute-start(bf16[1,4,128,128]{3,2,1,0:T(8,128)(2,1)S(1)} %get-tuple-element.41), channel_id=1, source_target_pairs={{0,2},{2,0},{4,6},{6,4},{8,10},{10,8},{12,14},{14,12},{1,3},{3,1},... | collective-permute-start | bytes 393224 | tf_op jit(solution)/shard_map/ppermute | solution.py:21
  4.7 1.3 %collective-permute-start.1 = (bf16[1,4,128,128]{3,2,1,0:T(8,128)(2,1)S(1)}, bf16[1,4,128,128]{3,2,1,0:T(8,128)(2,1)}, u32[]{:S(2)}, u32[]{:S(2)}) collective-permute-start(bf16[1,4,128,128]{3,2,1,0:T(8,128)(2,1)S(1)} %get-tuple-element.40), channel_id=1, source_target_pairs={{0,4},{2,6},{4,0},{6,2},{8,12},{10,14},{12,8},{14,10},{1,5},{3,7},... | collective-permute-start | bytes 393224 | tf_op jit(solution)/shard_map/ppermute | solution.py:21
  6.0 0.1 collective-permute-start.2
  6.2 0.0 collective-permute-start.3
  6.2 3.3 %collective-permute-start.4 = (bf16[1,4,128,128]{3,2,1,0:T(8,128)(2,1)S(1)}, bf16[1,4,128,128]{3,2,1,0:T(8,128)(2,1)S(1)}, u32[]{:S(2)}, u32[]{:S(2)}) collective-permute-start(bf16[1,4,128,128]{3,2,1,0:T(8,128)(2,1)S(1)} %get-tuple-element.37), channel_id=1, source_target_pairs={{0,10},{2,8},{4,14},{6,12},{8,2},{10,0},{12,6},{14,4},{1,11},{3,9}... | collective-permute-start | bytes 393224 | tf_op jit(solution)/shard_map/ppermute | solution.py:21
  9.5 0.0 copy-done.2
  9.5 0.3 multiply_convert_fusion
  9.8 0.3 fusion.53
  10.0 0.1 min.29
  10.1 0.0 copy-done.1
  10.2 0.1 lt.121
  10.3 0.0 collective-permute-done
  10.3 0.2 collective-permute-start.5
  10.5 0.9 %constant_dynamic-update-slice_fusion.6 = bf16[8,4,128,128]{3,2,1,0:T(8,128)(2,1)S(1)} fusion(bf16[8,4,128,128]{3,2,1,0:T(8,128)(2,1)S(1)} %get-tuple-element.42, bf16[1,4,128,128]{3,2,1,0:T(8,128)(2,1)} %collective-permute-done, s32[]{:T(128)S(6)} %select_n.105), kind=kLoop, calls=%fused_computation.79 | loop fusion | bytes 262148 | tf_op jit(solution)/shard_map/dynamic_update_slice | solution.py:22
  11.4 0.0 collective-permute-done.1
  11.4 1.3 %collective-permute-start.6 = (bf16[1,4,128,128]{3,2,1,0:T(8,128)(2,1)S(1)}, bf16[1,4,128,128]{3,2,1,0:T(8,128)(2,1)S(1)}, u32[]{:S(2)}, u32[]{:S(2)}) collective-permute-start(bf16[1,4,128,128]{3,2,1,0:T(8,128)(2,1)S(1)} %get-tuple-element.35), channel_id=1, source_target_pairs={{0,14},{2,12},{4,10},{6,8},{8,6},{10,4},{12,2},{14,0},{1,15},{3,13... | collective-permute-start | bytes 393224 | tf_op jit(solution)/shard_map/ppermute | solution.py:21
  12.7 0.9 %constant_dynamic-update-slice_fusion.5 = bf16[8,4,128,128]{3,2,1,0:T(8,128)(2,1)S(1)} fusion(bf16[8,4,128,128]{3,2,1,0:T(8,128)(2,1)S(1)} %constant_dynamic-update-slice_fusion.6, bf16[1,4,128,128]{3,2,1,0:T(8,128)(2,1)} %collective-permute-done.1, s32[]{:T(128)S(6)} %select_n.106), kind=kLoop, calls=%fused_computation.77 | loop fusion | bytes 262148 | tf_op jit(solution)/shard_map/dynamic_update_slice | solution.py:22
  13.6 0.1 collective-permute-done.2
  13.7 0.4 collective-permute-done.3
  14.2 2.8 %collective-permute-done.4 = bf16[1,4,128,128]{3,2,1,0:T(8,128)(2,1)S(1)} collective-permute-done((bf16[1,4,128,128]{3,2,1,0:T(8,128)(2,1)S(1)}, bf16[1,4,128,128]{3,2,1,0:T(8,128)(2,1)S(1)}, u32[]{:S(2)}, u32[]{:S(2)}) %collective-permute-start.4) | collective-permute-done | bytes 131104 | tf_op jit(solution)/shard_map/ppermute | solution.py:21
  17.0 10.6 %collective-permute-done.5 = bf16[1,4,128,128]{3,2,1,0:T(8,128)(2,1)S(1)} collective-permute-done((bf16[1,4,128,128]{3,2,1,0:T(8,128)(2,1)S(1)}, bf16[1,4,128,128]{3,2,1,0:T(8,128)(2,1)S(1)}, u32[]{:S(2)}, u32[]{:S(2)}) %collective-permute-start.5) | collective-permute-done | bytes 131104 | tf_op jit(solution)/shard_map/ppermute | solution.py:21
  27.6 4.4 %collective-permute-done.6 = bf16[1,4,128,128]{3,2,1,0:T(8,128)(2,1)S(1)} collective-permute-done((bf16[1,4,128,128]{3,2,1,0:T(8,128)(2,1)S(1)}, bf16[1,4,128,128]{3,2,1,0:T(8,128)(2,1)S(1)}, u32[]{:S(2)}, u32[]{:S(2)}) %collective-permute-start.6) | collective-permute-done | bytes 131104 | tf_op jit(solution)/shard_map/ppermute | solution.py:21
  32.0 0.7 %gather_fusion.1 = bf16[32,128,128]{2,1,0:T(8,128)(2,1)S(1)} fusion(bf16[32,128,128]{2,1,0:T(8,128)(2,1)S(1)} %bitcast.54, s32[1024]{0:T(1024)S(1)} %pad_clamp_fusion.1), kind=kCustom, calls=%fused_computation.1 | custom fusion | bytes 2097280 | tf_op jit(solution)/shard_map/gather | solution.py:105
  32.7 1.3 %convolution_convert_fusion = bf16[32,128,128]{2,1,0:T(8,128)(2,1)S(1)} fusion(bf16[32,128,128]{2,1,0:T(8,128)(2,1)S(1)} %gather_fusion.1, pred[32]{0:T(512)(128)(4,1)S(1)} %lt.121, f32[128]{0:T(128)S(1)} %iota_convert_fusion), kind=kOutput, calls=%fused_computation.11 | convolution fusion | flops 270303232 | bytes 2097696 | tf_op jit(solution)/shard_map/while/body/eval_jaxpr/bij,kj->bik/dot_general | solution.py:46
  34.1 5.8 %fusion.1 = f32[32,256,256]{2,1,0:T(8,128)} fusion(bf16[32,128,128]{2,1,0:T(8,128)(2,1)S(1)} %convolution_convert_fusion, bf16[128,128]{1,0:T(8,128)(2,1)S(1)} %get-tuple-element.45, bf16[128,128]{1,0:T(8,128)(2,1)S(1)} %get-tuple-element.46), kind=kOutput, calls=%fused_computation.6 | convolution fusion | flops 806617088 | bytes 9502720 | tf_op jit(solution)/shard_map/while/body/eval_jaxpr/bij,jk->bik/dot_general | solution.py:66
  39.8 4.4 %slice_subtract_fusion = (f32[32,128,128]{2,1,0:T(8,128)S(1)}, f32[32,128,128]{2,1,0:T(8,128)S(1)}) fusion(f32[32,256,256]{2,1,0:T(8,128)} %fusion.1), kind=kLoop, calls=%fused_computation.5 | loop fusion | flops 1572864 | bytes 12582912 | tf_op jit(solution)/shard_map/while/body/eval_jaxpr/sub | solution.py:67
  44.2 0.4 add_convert_fusion
  44.6 0.7 %fusion.9 = f32[16,256,256]{2,1,0:T(8,128)S(1)} fusion(bf16[16,128,128]{2,1,0:T(8,128)(2,1)S(1)} %get-tuple-element.34, bf16[16,128,128]{2,1,0:T(8,128)(2,1)S(1)} %get-tuple-element.33, bf16[128,128]{1,0:T(8,128)(2,1)S(1)} %get-tuple-element.46, bf16[128,128]{1,0:T(8,128)(2,1)S(1)} %get-tuple-element.45), kind=kOutput, calls=%fused_computation.18 | convolution fusion | flops 270663680 | bytes 5308416 | tf_op jit(solution)/shard_map/while/body/eval_jaxpr/bij,jk->bik/dot_general | solution.py:74
  45.3 0.3 fusion.8
  45.6 0.6 %multiply_reduce_fusion.1 = (f32[16]{0:T(128)S(1)}, f32[16]{0:T(128)S(1)}, f32[16]{0:T(128)S(1)}) fusion(f32[128]{0:T(128)S(1)} %compare_select_fusion.3, bf16[128,128]{1,0:T(8,128)(2,1)S(1)} %get-tuple-element.46, bf16[128,128]{1,0:T(8,128)(2,1)S(1)} %fusion.53, bf16[16,128,128]{2,1,0:T(8,128)(2,1)S(1)} %get-tuple-element.32, ...), kind=kOutput, calls=%fused_computation.26 | convolution fusion | flops 138018768 | bytes 1114816 | tf_op jit(solution)/shard_map/while/body/eval_jaxpr/ij,bjk->bik/dot_general | solution.py:78
  46.2 0.6 %pad_maximum_fusion.2 = f32[2,16]{1,0:T(2,128)} fusion(f32[1,16]{1,0:T(1,128)S(1)} %get-tuple-element.44, f32[1,16]{1,0:T(1,128)S(1)} %get-tuple-element.43), kind=kLoop, calls=%fused_computation.90 | loop fusion | flops 32 | bytes 256 | tf_op jit(solution)/shard_map/while/body/eval_jaxpr/stack | solution.py:83
  46.8 3.2 %all-gather = f32[2,16,2]{1,2,0:T(2,128)S(1)} all-gather(f32[1,16,2]{1,2,0:T(2,128)S(1)} %fusion.76), channel_id=1, replica_groups=mesh['parts'=2,'tiles'=8,'mesh'=2] {'mesh'}, dimensions={0}, use_global_device_ids=true | all-gather | bytes 384 | tf_op jit(solution)/shard_map/all_gather | solution.py:119
  50.0 0.1 copy.34
  50.1 1.0 %gather_fusion.2 = f32[512,2]{1,0:T(8,128)S(1)} fusion(f32[2,32]{0,1:T(8,128)S(1)} %bitcast.57, s32[1024]{0:T(1024)S(1)} %pad_clamp_fusion), kind=kCustom, calls=%fused_computation.2 | custom fusion | bytes 10240 | tf_op jit(solution)/shard_map/gather | solution.py:120
  51.1 0.1 copy.28
  51.2 0.6 %fusion.56 = f32[2,128]{1,0:T(2,128)} fusion(f32[2,4,128]{2,0,1:T(2,128)S(1)} %bitcast.59, f32[2,128]{1,0:T(2,128)S(1)} %slice_reduce_fusion), kind=kLoop, calls=%fused_computation.89 | loop fusion | flops 768 | bytes 3072 | tf_op jit(solution)/shard_map/add | solution.py:121
  (17 shorter events, 0.2 us)
Async XLA Ops:
  0.6 1.6 %copy-start = (bf16[32,128,128]{2,1,0:T(8,128)(2,1)S(1)}, bf16[32,128,128]{2,1,0:T(8,128)(2,1)}, u32[]{:S(2)}) copy-start(bf16[32,128,128]{2,1,0:T(8,128)(2,1)} %param.4) | copy-start | bytes 3145732
  3.1 6.4 %copy-start.2 = (s32[1,2,16]{2,1,0:T(2,128)S(1)}, s32[1,2,16]{2,1,0:T(2,128)}, u32[]{:S(2)}) copy-start(s32[1,2,16]{2,1,0:T(2,128)} %param.6) | copy-start | bytes 388
  3.1 7.0 %copy-start.1 = (s32[1,4,128]{2,1,0:T(4,128)S(1)}, s32[1,4,128]{2,1,0:T(4,128)}, u32[]{:S(2)}) copy-start(s32[1,4,128]{2,1,0:T(4,128)} %param.7) | copy-start | bytes 6148
  3.5 6.8 %collective-permute-start = (bf16[1,4,128,128]{3,2,1,0:T(8,128)(2,1)S(1)}, bf16[1,4,128,128]{3,2,1,0:T(8,128)(2,1)}, u32[]{:S(2)}, u32[]{:S(2)}) collective-permute-start(bf16[1,4,128,128]{3,2,1,0:T(8,128)(2,1)S(1)} %get-tuple-element.41), channel_id=1, source_target_pairs={{0,2},{2,0},{4,6},{6,4},{8,10},{10,8},{12,14},{14,12},{1,3},{3,1},... | collective-permute-start | bytes 393224 | tf_op jit(solution)/shard_map/ppermute | solution.py:21
  4.7 6.6 %collective-permute-start.1 = (bf16[1,4,128,128]{3,2,1,0:T(8,128)(2,1)S(1)}, bf16[1,4,128,128]{3,2,1,0:T(8,128)(2,1)}, u32[]{:S(2)}, u32[]{:S(2)}) collective-permute-start(bf16[1,4,128,128]{3,2,1,0:T(8,128)(2,1)S(1)} %get-tuple-element.40), channel_id=1, source_target_pairs={{0,4},{2,6},{4,0},{6,2},{8,12},{10,14},{12,8},{14,10},{1,5},{3,7},... | collective-permute-start | bytes 393224 | tf_op jit(solution)/shard_map/ppermute | solution.py:21
  6.0 7.7 %collective-permute-start.2 = (bf16[1,4,128,128]{3,2,1,0:T(8,128)(2,1)S(1)}, bf16[1,4,128,128]{3,2,1,0:T(8,128)(2,1)S(1)}, u32[]{:S(2)}, u32[]{:S(2)}) collective-permute-start(bf16[1,4,128,128]{3,2,1,0:T(8,128)(2,1)S(1)} %get-tuple-element.39), channel_id=1, source_target_pairs={{0,6},{2,4},{4,2},{6,0},{8,14},{10,12},{12,10},{14,8},{1,7},{3,5},... | collective-permute-start | bytes 393224 | tf_op jit(solution)/shard_map/ppermute | solution.py:21
  6.2 8.0 %collective-permute-start.3 = (bf16[1,4,128,128]{3,2,1,0:T(8,128)(2,1)S(1)}, bf16[1,4,128,128]{3,2,1,0:T(8,128)(2,1)S(1)}, u32[]{:S(2)}, u32[]{:S(2)}) collective-permute-start(bf16[1,4,128,128]{3,2,1,0:T(8,128)(2,1)S(1)} %get-tuple-element.38), channel_id=1, source_target_pairs={{0,8},{2,10},{4,12},{6,14},{8,0},{10,2},{12,4},{14,6},{1,9},{3,11}... | collective-permute-start | bytes 393224 | tf_op jit(solution)/shard_map/ppermute | solution.py:21
  6.2 10.8 %collective-permute-start.4 = (bf16[1,4,128,128]{3,2,1,0:T(8,128)(2,1)S(1)}, bf16[1,4,128,128]{3,2,1,0:T(8,128)(2,1)S(1)}, u32[]{:S(2)}, u32[]{:S(2)}) collective-permute-start(bf16[1,4,128,128]{3,2,1,0:T(8,128)(2,1)S(1)} %get-tuple-element.37), channel_id=1, source_target_pairs={{0,10},{2,8},{4,14},{6,12},{8,2},{10,0},{12,6},{14,4},{1,11},{3,9}... | collective-permute-start | bytes 393224 | tf_op jit(solution)/shard_map/ppermute | solution.py:21
  10.3 17.3 %collective-permute-start.5 = (bf16[1,4,128,128]{3,2,1,0:T(8,128)(2,1)S(1)}, bf16[1,4,128,128]{3,2,1,0:T(8,128)(2,1)S(1)}, u32[]{:S(2)}, u32[]{:S(2)}) collective-permute-start(bf16[1,4,128,128]{3,2,1,0:T(8,128)(2,1)S(1)} %get-tuple-element.36), channel_id=1, source_target_pairs={{0,12},{2,14},{4,8},{6,10},{8,4},{10,6},{12,0},{14,2},{1,13},{3,15... | collective-permute-start | bytes 393224 | tf_op jit(solution)/shard_map/ppermute | solution.py:21
  11.4 20.6 %collective-permute-start.6 = (bf16[1,4,128,128]{3,2,1,0:T(8,128)(2,1)S(1)}, bf16[1,4,128,128]{3,2,1,0:T(8,128)(2,1)S(1)}, u32[]{:S(2)}, u32[]{:S(2)}) collective-permute-start(bf16[1,4,128,128]{3,2,1,0:T(8,128)(2,1)S(1)} %get-tuple-element.35), channel_id=1, source_target_pairs={{0,14},{2,12},{4,10},{6,8},{8,6},{10,4},{12,2},{14,0},{1,15},{3,13... | collective-permute-start | bytes 393224 | tf_op jit(solution)/shard_map/ppermute | solution.py:21
